TPU v7x, 32 devices: a whole 2x2x4 slice. The times are simulated.
32 devices in a mesh: axial: 4 (over z), azim: 8 (over y, x, core).
Axes of the slice: x: 2, y: 2, z: 4, core: 2. Of those that a mesh axis runs over, the one named last changes fastest.
Arguments:
- fields: float32 [4096, 4, 1024], P(('axial', 'azim')), may hold values from -6 to 6
- new_owner: int32 [4096, 1], P(('axial', 'azim')), may hold values from 0 to 31; in each aligned block of 128 rows (0 to 127, 128 to 255, ...) at most 6 rows name the same one
- leaflet: bfloat16 [64, 128, 2048], P(None, 'axial', 'azim'), may hold values from -6 to 6
- stiffness: bfloat16 [64, 64], replicated, may hold values from -0.75 to 0.75
- coarse: float32 [2048, 256], P(('axial', 'azim')), may hold values from -6 to 6
- coarse_of_slot: int32 [6144], P(('axial', 'azim')), may hold values from 0 to 63
- viscosity: float32 [4], replicated, may hold values from 0.02 to 0.2
Outputs:
- regridded: float32 [6144, 4, 1024], P(('axial', 'azim'))
Inputs may be any that keep to these rules, and one draw needn't show every extreme that they name: `new_owner`: among the patches of one device, at most 6 share a new owner; in some device's patches exactly 6 do.
All inputs are finite; a program needn't handle non-finite values.
Results may differ from a plain program's by a relative error of at most 0.004.
Values may be sent and summed in bfloat16 or wider, within the bound.
A program may use at most 64 MiB of HBM per device.

v0:
```python
import functools
import jax
import jax.numpy as jnp
from jax import lax
from jax.experimental import pallas as pl
from jax.experimental.pallas import tpu as pltpu
from jax.sharding import PartitionSpec as P

PC = 64
FIELDS = 4
STEPS = 2
SPREAD = 0.25
LANES = 128
MESH = pl.DeviceIdType.MESH
F32 = jnp.float32
BF16 = jnp.bfloat16


def iota(shape, dim):
    return lax.broadcasted_iota(jnp.int32, shape, dim)


def peer(i, n_ax, n_az):
    j = i // n_az
    da = lax.rem(n_ax // 2 + ((j + 1) // 2) * (1 - 2 * lax.rem(j, 2)), n_ax)
    return da, lax.rem(lax.rem(i, n_az) + 1, n_az)


def send_kernel(
    n_ax, n_az, each, owner_hbm, slot_hbm, nu_hbm, fields_hbm, leaf_hbm, stiff_hbm, coarse_hbm, out_ref,
    owner_ref, slot_ref, nu_ref, fields_ref, leaf_ref, stiff_ref, coarse_ref, load_sem,
    rows_f, cols_f, edge_rows, edge_cols, got_rows, got_cols, lap_ref, forced_ref, packed_ref,
    landed_ref, strip_ref, pick_row, pick_ref,
    halo_send, halo_recv, send_sem, recv_sem, pick_sem, closed_sem,
):
    a = lax.axis_index("axial")
    z = lax.axis_index("azim")
    me = a * n_az + z
    devices = n_ax * n_az
    records, rows, cols = leaf_ref.shape
    patches, height, _ = fields_ref.shape
    blocks = rows // 8

    pairs_in = (
        (leaf_hbm, leaf_ref), (stiff_hbm, stiff_ref), (owner_hbm, owner_ref), (coarse_hbm, coarse_ref),
        (slot_hbm, slot_ref), (nu_hbm, nu_ref), (fields_hbm, fields_ref),
    )
    loads = [
        pltpu.make_async_copy(src, dst, load_sem.at[i]) for i, (src, dst) in enumerate(pairs_in)
    ]
    for load in loads:
        load.start()
    got_rows[...] = jnp.zeros_like(got_rows)
    barrier = pltpu.get_barrier_semaphore()

    row_peers = [(a, lax.rem(z + dz, n_az)) for dz in range(1, n_az)]
    column_peers = [(lax.rem(a + da, n_ax), z) for da in range(1, n_ax)]
    for other in row_peers + column_peers:
        pl.semaphore_signal(barrier, inc=1, device_id=other, device_id_type=MESH)

    row_id = iota((rows, LANES), 0)
    lane_id = iota((rows, LANES), 1)
    eye_low = lane_id == row_id
    eye_high = lane_id == row_id + rows

    def edges(k, carry):
        x = leaf_ref[k].astype(F32)
        rows_f[0, pl.ds(k, 1), :] = x[0:1, :]
        rows_f[1, pl.ds(k, 1), :] = x[rows - 1:rows, :]
        first = jnp.broadcast_to(x[:, 0:1], (rows, LANES))
        last = jnp.broadcast_to(x[:, cols - 1:cols], (rows, LANES))
        both = jnp.where(eye_low, first, jnp.where(eye_high, last, 0.0))
        cols_f[pl.ds(k, 1), :] = jnp.sum(both, axis=0, keepdims=True)
        return carry

    loads[0].wait()
    lax.fori_loop(0, records, edges, 0, unroll=4)
    edge_rows[...] = rows_f[...].astype(BF16)
    edge_cols[...] = cols_f[...].astype(BF16)
    wide_row = iota((rows, cols), 0)
    wide_lane = iota((rows, cols), 1)

    def laplace(k, carry):
        x = leaf_ref[k].astype(F32)
        north = jnp.where(wide_row == 0, 0.0, pltpu.roll(x, 1, 0))
        south = jnp.where(wide_row == rows - 1, 0.0, pltpu.roll(x, rows - 1, 0))
        west = jnp.where(wide_lane == 0, 0.0, pltpu.roll(x, 1, 1))
        east = jnp.where(wide_lane == cols - 1, 0.0, pltpu.roll(x, cols - 1, 1))
        total = south + north + west + east - 4.0 * x
        for b in range(blocks):
            lap_ref[b, pl.ds(pl.multiple_of(k * 8, 8), 8), :] = total[b * 8:(b + 1) * 8, :]
        return carry

    lax.fori_loop(0, records // 2, laplace, 0, unroll=4)
    pl.semaphore_wait(barrier, len(row_peers) + len(column_peers))
    for other in row_peers:
        pl.semaphore_signal(closed_sem, inc=1, device_id=other, device_id_type=MESH)

    def halo(src, dst, i, device):
        return pltpu.make_async_remote_copy(
            src_ref=src, dst_ref=dst, send_sem=halo_send.at[i], recv_sem=halo_recv.at[i],
            device_id=device, device_id_type=MESH,
        )

    down = halo(edge_rows.at[1], got_rows.at[0], 0, (lax.rem(a + 1, n_ax), z))
    up = halo(edge_rows.at[0], got_rows.at[1], 1, (lax.rem(a + n_ax - 1, n_ax), z))
    right = halo(edge_cols, got_cols.at[0], 2, (a, lax.rem(z + 1, n_az)))
    left = halo(edge_cols, got_cols.at[1], 3, (a, lax.rem(z + n_az - 1, n_az)))

    @pl.when(a < n_ax - 1)
    def _():
        down.start()

    @pl.when(a > 0)
    def _():
        up.start()

    right.start()
    left.start()

    lax.fori_loop(records // 2, records, laplace, 0, unroll=4)
    for load in loads[1:6]:
        load.wait()
    pairs = records // FIELDS // 2
    width = pairs * FIELDS
    big = 8 * records
    out_row = iota((big, records), 0)
    record = iota((big, records), 1)
    within = lax.rem(out_row, width)
    wanted = lax.rem(within, FIELDS) * (2 * pairs) + 2 * (within // FIELDS) + out_row // (8 * width)
    row_pick = (record == wanted).astype(BF16)
    col_pick = (iota((records, big), 0) == iota((records, big), 1) // 8).astype(BF16)
    spread = jnp.dot(stiff_ref[...], col_pick, preferred_element_type=F32).astype(BF16)
    spread = jnp.dot(row_pick, spread, preferred_element_type=F32)
    same = lax.rem(iota((big, big), 0) // width, 8) == lax.rem(iota((big, big), 1), 8)
    law = jnp.where(same, spread, 0.0).astype(BF16)
    forced_ref[patches] = jnp.zeros(forced_ref.shape[1:], BF16)
    pick_slots(each, owner_ref, pick_row)
    picked = pltpu.make_async_copy(pick_row, pick_ref, pick_sem)
    picked.start()
    interpolate(coarse_ref, strip_ref)

    @pl.when(a > 0)
    def _():
        down.wait_recv()

    @pl.when(a < n_ax - 1)
    def _():
        up.wait_recv()

    right.wait_recv()
    left.wait_recv()
    rows_f2 = got_rows[...].astype(F32)
    cols_l = got_cols[0].astype(F32)
    cols_r = got_cols[1].astype(F32)

    @pl.when(a < n_ax - 1)
    def _():
        down.wait_send()

    @pl.when(a > 0)
    def _():
        up.wait_send()

    right.wait_send()
    left.wait_send()
    rows_f[...] = rows_f2
    cols_f[...] = jnp.where(iota(cols_l.shape, 1) < rows, cols_r, cols_l)
    first_row = iota((8, cols), 0) == 0
    last_row = iota((8, cols), 0) == 7
    first_lane = lane_id == 0
    last_lane = lane_id == LANES - 1

    def sides(k, carry):
        halo_cols = jnp.broadcast_to(cols_f[pl.ds(k, 1), :], (rows, LANES))
        after = jnp.sum(jnp.where(eye_low, halo_cols, 0.0), axis=1, keepdims=True)
        before = jnp.sum(jnp.where(eye_high, halo_cols, 0.0), axis=1, keepdims=True)
        west = jnp.where(first_lane, before, 0.0)
        east = jnp.where(last_lane, after, 0.0)
        here = pl.ds(pl.multiple_of(k * 8, 8), 8)
        lap_ref[0, here, :] += jnp.where(first_row, rows_f[0, pl.ds(k, 1), :], 0.0)
        lap_ref[blocks - 1, here, :] += jnp.where(last_row, rows_f[1, pl.ds(k, 1), :], 0.0)
        for b in range(blocks):
            lap_ref[b, here, :LANES] += west[b * 8:(b + 1) * 8]
            lap_ref[b, here, cols - LANES:] += east[b * 8:(b + 1) * 8]
        return carry

    lax.fori_loop(0, records, sides, 0, unroll=8)
    loads[6].wait()
    low = iota((width, LANES), 1) < PC
    across = cols // PC

    def force(b, carry):
        tension = jnp.dot(law, lap_ref[b].astype(BF16), preferred_element_type=F32)
        tension = tension.astype(BF16).astype(F32) * SPREAD
        for r in range(8):
            for t in range(cols // LANES):
                even = tension[r * width:(r + 1) * width, t * LANES:(t + 1) * LANES]
                odd = tension[(8 + r) * width:(9 + r) * width, t * LANES:(t + 1) * LANES]
                p = (b * 8 + r) * across + 2 * t
                first = jnp.where(low, even, pltpu.roll(odd, PC, 1))
                second = jnp.where(low, pltpu.roll(even, PC, 1), odd)
                forced_ref[p] = (fields_ref[p] + first).astype(BF16)
                forced_ref[p + 1] = (fields_ref[p + 1] + second).astype(BF16)
        return carry

    lax.fori_loop(0, blocks, force, 0)

    picked.wait()
    pl.semaphore_wait(closed_sem, len(row_peers))

    def outgoing(i):
        da, dz = peer(i, n_ax, n_az)
        ta, tz = lax.rem(a + da, n_ax), lax.rem(z + dz, n_az)
        other = ta * n_az + tz
        return other, pltpu.make_async_remote_copy(
            src_ref=packed_ref.at[other], dst_ref=landed_ref.at[me],
            send_sem=send_sem.at[i], recv_sem=recv_sem.at[i],
            device_id=(ta, tz), device_id_type=MESH,
        )

    def send(i, carry):
        other, copy = outgoing(i)
        for k in range(each):
            packed_ref[other, k] = forced_ref[pick_ref[0, other * each + k]]
        copy.start()
        return carry

    lax.fori_loop(0, devices - 1, send, 0)

    row = iota((height, LANES), 0)
    nu = jnp.full((height, LANES), nu_ref[0], F32)
    for f in range(1, FIELDS):
        nu = jnp.where(lax.rem(row, FIELDS) == f, nu_ref[f], nu)

    for k in range(each):
        ghost = strip_ref[slot_ref[me * each + k]]
        block = forced_ref[pick_ref[0, me * each + k]].astype(F32)
        out_ref[me, k] = relax(block, ghost, nu)

    def arrive(turn, carry):
        i = lax.rem(turn + devices - n_az, devices - 1)
        da, dz = peer(i, n_ax, n_az)
        source = lax.rem(a + n_ax - da, n_ax) * n_az + lax.rem(z + n_az - dz, n_az)
        pltpu.make_async_remote_copy(
            src_ref=packed_ref.at[source], dst_ref=landed_ref.at[source],
            send_sem=send_sem.at[i], recv_sem=recv_sem.at[i],
            device_id=(a, z), device_id_type=MESH,
        ).wait_recv()
        for k in range(each):
            ghost = strip_ref[slot_ref[source * each + k]]
            out_ref[source, k] = relax(landed_ref[source, k].astype(F32), ghost, nu)
        return carry

    lax.fori_loop(0, devices - 1, arrive, 0)

    def finish(i, carry):
        outgoing(i)[1].wait_send()
        return carry

    lax.fori_loop(0, devices - 1, finish, 0)


def pick_slots(each, owner_ref, pick_row):
    patches = owner_ref.shape[1]
    slots = pick_row.shape[1]
    square = (patches, patches)
    eye = iota(square, 0) == iota(square, 1)
    owner = owner_ref[...]
    across = jnp.broadcast_to(owner, square)
    along = jnp.sum(jnp.where(eye, across, 0), axis=1, keepdims=True)
    earlier = (along == across) & (iota(square, 0) < iota(square, 1))
    rank = jnp.sum(earlier.astype(jnp.int32), axis=0, keepdims=True)
    target = jnp.broadcast_to(owner * each + rank, square)
    target = jnp.sum(jnp.where(eye, target, 0), axis=1, keepdims=True)
    shape = (patches, slots)
    taken = target == iota(shape, 1)
    pick_row[...] = patches + jnp.sum(
        jnp.where(taken, iota(shape, 0) - patches, 0), axis=0, keepdims=True
    )


def interpolate(coarse_ref, strip_ref):
    fine = iota((PC, LANES), 1)
    src = iota((PC, LANES), 0)
    cell = lax.rem(fine, PC)
    near = (fine // PC) * (PC // 2) + cell // 2
    second = jnp.where(
        lax.rem(fine, 2) == 0,
        jnp.where(cell == 0, near, near - 1),
        jnp.where(cell == PC - 1, near, near + 1),
    )
    table = (0.75 * (src == near).astype(F32) + 0.25 * (src == second).astype(F32)).astype(BF16)
    for f in range(FIELDS):
        raw = coarse_ref[:, f * PC:(f + 1) * PC]
        top = raw.astype(BF16)
        rest = (raw - top.astype(F32)).astype(BF16)
        fine_cells = jnp.dot(top, table, preferred_element_type=F32)
        fine_cells = fine_cells + jnp.dot(rest, table, preferred_element_type=F32)
        strip_ref[:, f, :] = fine_cells
        strip_ref[:, FIELDS + f, :] = fine_cells


def relax(state, ghost, nu):
    shape = (8, LANES)
    lane = iota(shape, 1)
    low = iota(shape, 0) < FIELDS
    cell = lax.rem(lane, PC)
    up = (lane < PC) & low
    down = (lane >= PC) & (iota(shape, 0) >= FIELDS)
    count = state.shape[0] // 8
    tiles = [state[8 * j:8 * j + 8] for j in range(count)]
    for _ in range(STEPS):
        swap = [pltpu.roll(t, PC, 1) for t in tiles]
        turned = [ghost] + [pltpu.roll(t, FIELDS, 0) for t in swap] + [ghost]
        fresh = []
        for j, t in enumerate(tiles):
            beyond = jnp.where(up, turned[j], jnp.where(down, turned[j + 2], turned[j + 1]))
            west = jnp.where(cell == 0, 0.0, pltpu.roll(t, 1, 1))
            east = jnp.where(cell == PC - 1, 0.0, pltpu.roll(t, LANES - 1, 1))
            total = swap[j] + beyond + west + east - 4.0 * t
            fresh.append(t + nu[8 * j:8 * j + 8] * total)
        tiles = fresh
    return jnp.concatenate(tiles, axis=0)


def shards(mesh, fields, new_owner, leaflet, stiffness, coarse, coarse_of_slot, viscosity):
    n_ax, n_az = mesh.shape["axial"], mesh.shape["azim"]
    devices = n_ax * n_az
    patches, _, section = fields.shape
    records, rows, cols = leaflet.shape
    each = max(2, 3 * patches // (2 * devices))
    slots = devices * each
    wide = -(-slots // LANES) * LANES
    height = FIELDS * section // LANES
    view = fields.reshape(patches, FIELDS, section // LANES, LANES).transpose(0, 2, 1, 3)
    view = view.reshape(patches, height, LANES)
    given = (new_owner.reshape(1, patches), coarse_of_slot, viscosity, view, leaflet, stiffness, coarse)
    out = pl.pallas_call(
        functools.partial(send_kernel, n_ax, n_az, each),
        out_shape=pltpu.VMEM((devices, each, height, LANES), F32),
        in_specs=[pl.BlockSpec(memory_space=pltpu.HBM)] * 7,
        out_specs=pl.BlockSpec(memory_space=pltpu.VMEM),
        scratch_shapes=[
            pltpu.VMEM((1, patches), jnp.int32),
            pltpu.SMEM((slots,), jnp.int32),
            pltpu.SMEM((FIELDS,), F32),
            pltpu.VMEM((patches, height, LANES), F32),
            pltpu.VMEM(leaflet.shape, BF16),
            pltpu.VMEM(stiffness.shape, BF16),
            pltpu.VMEM(coarse.shape, F32),
            pltpu.SemaphoreType.DMA((7,)),
            pltpu.VMEM((2, records, cols), F32),
            pltpu.VMEM((records, LANES), F32),
            pltpu.VMEM((2, records, cols), BF16),
            pltpu.VMEM((records, LANES), BF16),
            pltpu.VMEM((2, records, cols), BF16),
            pltpu.VMEM((2, records, LANES), BF16),
            pltpu.VMEM((rows // 8, 8 * records, cols), F32),
            pltpu.VMEM((patches + 1, height, LANES), BF16),
            pltpu.VMEM((devices, each, height, LANES), BF16),
            pltpu.VMEM((devices, each, height, LANES), BF16),
            pltpu.VMEM((coarse.shape[0], 2 * FIELDS, LANES), F32),
            pltpu.VMEM((1, wide), jnp.int32),
            pltpu.SMEM((1, wide), jnp.int32),
            pltpu.SemaphoreType.DMA((4,)),
            pltpu.SemaphoreType.DMA((4,)),
            pltpu.SemaphoreType.DMA((devices - 1,)),
            pltpu.SemaphoreType.DMA((devices - 1,)),
            pltpu.SemaphoreType.DMA,
            pltpu.SemaphoreType.REGULAR,
        ],
        compiler_params=pltpu.CompilerParams(
            collective_id=0, has_side_effects=True, vmem_limit_bytes=40 << 20
        ),
        name="regrid",
    )(*[pltpu.with_memory_space_constraint(v, pltpu.HBM) for v in given])
    out = out.reshape(slots, section // LANES, FIELDS, LANES).transpose(0, 2, 1, 3)
    return out.reshape(slots, FIELDS, section)


def solution(mesh):
    placed = (
        P(("axial", "azim"), None, None),
        P(("axial", "azim"), None),
        P(None, "axial", "azim"),
        P(),
        P(("axial", "azim"), None),
        P(("axial", "azim")),
        P(),
    )
    return jax.shard_map(
        functools.partial(shards, mesh),
        mesh=mesh,
        in_specs=placed,
        out_specs=P(("axial", "azim"), None, None),
        check_vma=False,
    )
```

profile of v0, /device:TPU:11, one launch (start us, length us, event | category | flops | bytes accessed | tf_op | source)
XLA Modules:
  0.0 49.5 jit_solution(18043851597195451351)
XLA Ops:
  0.0 47.8 %regrid.1 = f32[32,6,32,128]{3,2,1,0:T(8,128)S(1)} custom-call(s32[1,128]{1,0:T(1,128)} %bitcast.13, s32[192]{0:T(256)} %slot_hbm.1, f32[4]{0:T(128)} %nu_hbm.1, f32[128,32,128]{2,1,0:T(8,128)} %bitcast.12, bf16[64,32,256]{2,1,0:T(8,128)(2,1)} %leaf_hbm.1, bf16[64,64]{1,0:T(8,128)(2,1)} %stiff_hbm.1, f32[64,256]{1,0:T(8,128)} %coarse_hbm.1), custom_call_target="tpu_custom_call" | custom-call | tf_op jit(solution)/shard_map/regrid/pallas_call | solution.py:339
  47.8 1.7 %copy.11 = f32[192,4,1024]{2,1,0:T(4,128)} copy(f32[192,4,1024]{2,1,0:T(4,128)S(1)} %bitcast.11) | data formatting | bytes 6291456
where the time goes:
time: 50.3 us; the launch traced here: 49.5 us
  Pallas kernels  47.8 us (95%)
  local copies, waits for them, and re-layouts  1.67 us (3%)
    pallas_call x1, Pallas kernels, shards(): pl.pallas_call(functools.partial(send_kernel, n_ax, n_az, each), out_shap...  47.8 us
    unnamed x1, local copies, waits for them, and re-layouts  1.67 us

commit v1 on v0

v1 whole, which is shorter than its diff:
```python
import functools
import jax
import jax.numpy as jnp
from jax import lax
from jax.experimental import pallas as pl
from jax.experimental.pallas import tpu as pltpu
from jax.sharding import PartitionSpec as P

PC = 64
FIELDS = 4
STEPS = 2
SPREAD = 0.25
PHASES = 2
BAND = 16
TOGETHER = 4
LANES = 128
MESH = pl.DeviceIdType.MESH
F32 = jnp.float32
BF16 = jnp.bfloat16


def iota(shape, dim):
    return lax.broadcasted_iota(jnp.int32, shape, dim)


def shifts(n_ax):
    if n_ax & (n_ax - 1):
        away = [n_ax // 2 + ((j + 1) // 2) * (1 - 2 * (j % 2)) for j in range(n_ax)]
        return [d % n_ax for d in away]
    return [k ^ (k >> 1) for k in reversed(range(n_ax))]


def partner(a, shift, n_ax, back=False):
    if n_ax & (n_ax - 1):
        return lax.rem(a + (n_ax - shift if back else shift), n_ax)
    return a ^ shift


def send_kernel(
    n_ax, n_az, each, owner_hbm, slot_hbm, nu_hbm, fields_hbm, leaf_hbm, stiff_hbm, coarse_hbm, out_ref,
    owner_ref, slot_ref, nu_ref, fields_ref, leaf_ref, stiff_ref, coarse_ref, load_sem,
    edge_rows, edge_cols, got_rows, got_cols, law_ref, side_ref, coupled_ref, forced_ref, packed_ref,
    landed_ref, strip_ref, pick_row, pick_ref,
    halo_send, halo_recv, send_sem, recv_sem, pick_sem, closed_sem,
):
    a = lax.axis_index("axial")
    z = lax.axis_index("azim")
    me = a * n_az + z
    devices = n_ax * n_az
    records, rows, cols = leaf_ref.shape
    patches, height, _ = fields_ref.shape
    blocks = rows // BAND
    deep = records * BAND
    pairs = records // FIELDS // 2
    share = pairs // PHASES * FIELDS
    wide = 2 * share

    pairs_in = (
        (owner_hbm, owner_ref), (stiff_hbm, stiff_ref), (leaf_hbm, leaf_ref), (fields_hbm, fields_ref),
        (coarse_hbm, coarse_ref), (slot_hbm, slot_ref), (nu_hbm, nu_ref),
    )
    loads = [
        pltpu.make_async_copy(src, dst, load_sem.at[i]) for i, (src, dst) in enumerate(pairs_in)
    ]
    for load in loads:
        load.start()
    got_rows[...] = jnp.zeros_like(got_rows)
    barrier = pltpu.get_barrier_semaphore()

    row_peers = [(a, lax.rem(z + dz, n_az)) for dz in range(1, n_az)]
    column_peers = [(lax.rem(a + da, n_ax), z) for da in range(1, n_ax)]
    for other in row_peers + column_peers:
        pl.semaphore_signal(barrier, inc=1, device_id=other, device_id_type=MESH)

    column = iota((records, deep), 1)
    belongs = iota((records, deep), 0) == column // BAND
    gather = belongs.astype(BF16)
    gather_first = (belongs & (lax.rem(column, BAND) == 0)).astype(BF16)
    gather_last = (belongs & (lax.rem(column, BAND) == BAND - 1)).astype(BF16)
    source = iota((cols, LANES), 0)
    odd_lane = lax.rem(iota((cols, LANES), 1), 2) == 1
    ends = (((source == cols - 1) & ~odd_lane) | ((source == 0) & odd_lane)).astype(BF16)

    loads[0].wait()
    pick_slots(each, owner_ref, pick_row)
    picked = pltpu.make_async_copy(pick_row, pick_ref, pick_sem)
    picked.start()
    forced_ref[patches] = jnp.zeros(forced_ref.shape[1:], BF16)

    loads[1].wait()
    spread = jnp.dot(stiff_ref[...], gather, preferred_element_type=F32).astype(BF16)
    row_of = lax.rem(iota((wide, deep), 1), BAND)
    small = []
    for h in range(PHASES):
        order = iota((wide, records), 0)
        within = lax.rem(order, share)
        wanted = lax.rem(within, FIELDS) * (2 * pairs) + order // share
        wanted = wanted + 2 * (h * (pairs // PHASES) + within // FIELDS)
        chosen = (iota((wide, records), 1) == wanted).astype(BF16)
        small.append(jnp.dot(chosen, stiff_ref[...], preferred_element_type=F32).astype(BF16))
        base = jnp.dot(chosen, spread, preferred_element_type=F32)

        def fill(r, carry, h=h, base=base):
            here = pl.ds(pl.multiple_of(r * wide, wide), wide)
            law_ref[h, here, :] = jnp.where(row_of == r, base, 0.0).astype(BF16)
            return carry

        lax.fori_loop(0, BAND, fill, 0, unroll=2)

    loads[2].wait()
    band_lane = iota((BAND, LANES), 1)
    band_row = iota((BAND, LANES), 0)

    def band(b):
        return leaf_ref[:, pl.ds(pl.multiple_of(b * BAND, BAND), BAND), :].reshape(deep, cols)

    total = jnp.zeros((records, LANES), F32)
    for b in range(blocks):
        both = jnp.dot(band(b), ends, preferred_element_type=F32).reshape(records, BAND, LANES)
        twice = 2 * (band_row + b * BAND)
        kept = (band_lane == twice) | (band_lane == lax.rem(twice + LANES - 1, LANES))
        both = jnp.where(kept[None], both, 0.0).astype(BF16).reshape(deep, LANES)
        total = total + jnp.dot(gather, both, preferred_element_type=F32)
    edge_cols[...] = total.astype(BF16)
    edge_rows[0] = jnp.dot(gather_first, band(0), preferred_element_type=F32).astype(BF16)
    edge_rows[1] = jnp.dot(gather_last, band(blocks - 1), preferred_element_type=F32).astype(BF16)

    pl.semaphore_wait(barrier, len(row_peers) + len(column_peers))
    for other in row_peers:
        pl.semaphore_signal(closed_sem, inc=1, device_id=other, device_id_type=MESH)

    def halo(src, dst, i, device):
        return pltpu.make_async_remote_copy(
            src_ref=src, dst_ref=dst, send_sem=halo_send.at[i], recv_sem=halo_recv.at[i],
            device_id=device, device_id_type=MESH,
        )

    down = halo(edge_rows.at[1], got_rows.at[0], 0, (lax.rem(a + 1, n_ax), z))
    up = halo(edge_rows.at[0], got_rows.at[1], 1, (lax.rem(a + n_ax - 1, n_ax), z))
    right = halo(edge_cols, got_cols.at[0], 2, (a, lax.rem(z + 1, n_az)))
    left = halo(edge_cols, got_cols.at[1], 3, (a, lax.rem(z + n_az - 1, n_az)))

    @pl.when(a < n_ax - 1)
    def _():
        down.start()

    @pl.when(a > 0)
    def _():
        up.start()

    right.start()
    left.start()

    def couple(h):
        def one(b, carry):
            found = jnp.dot(law_ref[h], band(b), preferred_element_type=F32)
            coupled_ref[h, pl.ds(1 + b * BAND, BAND)] = found.reshape(BAND, wide, cols)
            return carry

        lax.fori_loop(0, blocks, one, 0)

    couple(0)

    @pl.when(a > 0)
    def _():
        down.wait_recv()

    @pl.when(a < n_ax - 1)
    def _():
        up.wait_recv()

    right.wait_recv()
    left.wait_recv()
    even = lax.rem(iota((records, LANES), 1), 2) == 0
    beside = jnp.where(even, got_cols[0].astype(F32), got_cols[1].astype(F32)).astype(BF16)

    def border(h):
        side_ref[h] = jnp.dot(small[h], beside, preferred_element_type=F32)
        coupled_ref[h, 0] = jnp.dot(small[h], got_rows[0], preferred_element_type=F32)
        coupled_ref[h, rows + 1] = jnp.dot(small[h], got_rows[1], preferred_element_type=F32)

    border(0)

    lane = iota((wide, LANES), 1)
    first_lane = lane == 0
    last_lane = lane == LANES - 1
    low = iota((share, LANES), 1) < PC
    across = cols // PC
    tiles = cols // LANES

    def force(h):
        part = slice(h * share, (h + 1) * share)

        def some(turn, carry):
            stored = []
            for r in [turn * TOGETHER + n for n in range(TOGETHER)]:
                beyond = pltpu.roll(side_ref[h], lax.rem(2 * LANES - 2 * r, LANES), 1)
                here = [coupled_ref[h, r + 1, :, t * LANES:(t + 1) * LANES] for t in range(tiles)]
                west = [pltpu.roll(v, 1, 1) for v in here]
                east = [pltpu.roll(v, LANES - 1, 1) for v in here]
                for t in range(tiles):
                    cut = slice(t * LANES, (t + 1) * LANES)
                    before = west[t - 1] if t else beyond
                    after = east[t + 1] if t < tiles - 1 else beyond
                    sums = jnp.where(first_lane, before, west[t]) + jnp.where(last_lane, after, east[t])
                    sums = sums + (coupled_ref[h, r, :, cut] + coupled_ref[h, r + 2, :, cut])
                    change = SPREAD * sums - (4.0 * SPREAD) * here[t]
                    top, bottom = change[:share], change[share:]
                    turned = pltpu.roll(jnp.where(low, bottom, top), PC, 1)
                    p = r * across + 2 * t
                    stored.append((p, (fields_ref[p, part] + jnp.where(low, top, turned)).astype(BF16)))
                    stored.append((p + 1, (fields_ref[p + 1, part] + jnp.where(low, turned, bottom)).astype(BF16)))
            for p, value in stored:
                forced_ref[p, part] = value
            return carry

        lax.fori_loop(0, rows // TOGETHER, some, 0)

    order = shifts(n_ax)
    turns = [n_az - (shift == 0) for shift in order]

    def piece(ref, at, h):
        return ref.at[at] if h is None else ref.at[at, :, h * share:(h + 1) * share]

    def outgoing(j, d, h=None):
        ta, tz = partner(a, order[j], n_ax), lax.rem(z + d + 1, n_az)
        other = ta * n_az + tz
        return other, pltpu.make_async_remote_copy(
            src_ref=piece(packed_ref, other, h), dst_ref=piece(landed_ref, me, h),
            send_sem=send_sem.at[h or 0, j * n_az + d], recv_sem=recv_sem.at[h or 0, j * n_az + d],
            device_id=(ta, tz), device_id_type=MESH,
        )

    def incoming(j, d, h=None):
        source = partner(a, order[j], n_ax, back=True) * n_az + lax.rem(z + n_az - d - 1, n_az)
        return source, pltpu.make_async_remote_copy(
            src_ref=piece(packed_ref, source, h), dst_ref=piece(landed_ref, source, h),
            send_sem=send_sem.at[h or 0, j * n_az + d], recv_sem=recv_sem.at[h or 0, j * n_az + d],
            device_id=(a, z), device_id_type=MESH,
        )

    def send_all(j, h=None):
        part = slice(None) if h is None else slice(h * share, (h + 1) * share)

        def send(d, carry):
            other, copy = outgoing(j, d, h)
            for k in range(each):
                packed_ref[other, k, part] = forced_ref[pick_ref[0, other * each + k], part]
            copy.start()
            return carry

        lax.fori_loop(0, turns[j], send, 0)

    halves = [range(PHASES) if j == 0 else (None,) for j in range(n_ax)]

    loads[3].wait()
    force(0)
    picked.wait()
    pl.semaphore_wait(closed_sem, len(row_peers))
    send_all(0, 0)
    for h in range(1, PHASES):
        couple(h)
        border(h)
        force(h)
        send_all(0, h)
    for j in range(1, n_ax):
        send_all(j)

    for load in loads[4:]:
        load.wait()
    interpolate(coarse_ref, strip_ref)
    row = iota((height, LANES), 0)
    nu = jnp.full((height, LANES), nu_ref[0], F32)
    for f in range(1, FIELDS):
        nu = jnp.where(lax.rem(row, FIELDS) == f, nu_ref[f], nu)

    for k in range(each):
        ghost = strip_ref[slot_ref[me * each + k]]
        block = forced_ref[pick_ref[0, me * each + k]].astype(F32)
        out_ref[me, k] = relax(block, ghost, nu)

    def arrive(j, d):
        for h in halves[j]:
            source, copy = incoming(j, d, h)
            copy.wait_recv()
        for k in range(each):
            ghost = strip_ref[slot_ref[source * each + k]]
            out_ref[source, k] = relax(landed_ref[source, k].astype(F32), ghost, nu)

    far = n_ax // 2
    for j in sorted(range(n_ax), key=lambda j: (order[j] > 0, order[j] != far, order[j] > far, -order[j])):
        def one(d, carry, j=j):
            arrive(j, d)
            return carry

        lax.fori_loop(0, turns[j], one, 0)

    for j in range(n_ax):
        def finish(d, carry, j=j):
            for h in halves[j]:
                outgoing(j, d, h)[1].wait_send()
            return carry

        lax.fori_loop(0, turns[j], finish, 0)

    @pl.when(a < n_ax - 1)
    def _():
        down.wait_send()

    @pl.when(a > 0)
    def _():
        up.wait_send()

    right.wait_send()
    left.wait_send()


def pick_slots(each, owner_ref, pick_row):
    patches = owner_ref.shape[1]
    slots = pick_row.shape[1]
    square = (patches, patches)
    eye = iota(square, 0) == iota(square, 1)
    owner = owner_ref[...]
    across = jnp.broadcast_to(owner, square)
    along = jnp.sum(jnp.where(eye, across, 0), axis=1, keepdims=True)
    earlier = (along == across) & (iota(square, 0) < iota(square, 1))
    rank = jnp.sum(earlier.astype(jnp.int32), axis=0, keepdims=True)
    target = jnp.broadcast_to(owner * each + rank, square)
    target = jnp.sum(jnp.where(eye, target, 0), axis=1, keepdims=True)
    shape = (patches, slots)
    taken = target == iota(shape, 1)
    pick_row[...] = patches + jnp.sum(
        jnp.where(taken, iota(shape, 0) - patches, 0), axis=0, keepdims=True
    )


def interpolate(coarse_ref, strip_ref):
    fine = iota((PC, LANES), 1)
    src = iota((PC, LANES), 0)
    cell = lax.rem(fine, PC)
    near = (fine // PC) * (PC // 2) + cell // 2
    second = jnp.where(
        lax.rem(fine, 2) == 0,
        jnp.where(cell == 0, near, near - 1),
        jnp.where(cell == PC - 1, near, near + 1),
    )
    table = (0.75 * (src == near).astype(F32) + 0.25 * (src == second).astype(F32)).astype(BF16)
    for f in range(FIELDS):
        raw = coarse_ref[:, f * PC:(f + 1) * PC]
        top = raw.astype(BF16)
        rest = (raw - top.astype(F32)).astype(BF16)
        fine_cells = jnp.dot(top, table, preferred_element_type=F32)
        fine_cells = fine_cells + jnp.dot(rest, table, preferred_element_type=F32)
        strip_ref[:, f, :] = fine_cells
        strip_ref[:, FIELDS + f, :] = fine_cells


def relax(state, ghost, nu):
    shape = (8, LANES)
    lane = iota(shape, 1)
    low = iota(shape, 0) < FIELDS
    cell = lax.rem(lane, PC)
    up = (lane < PC) & low
    down = (lane >= PC) & (iota(shape, 0) >= FIELDS)
    count = state.shape[0] // 8
    tiles = [state[8 * j:8 * j + 8] for j in range(count)]
    for _ in range(STEPS):
        swap = [pltpu.roll(t, PC, 1) for t in tiles]
        turned = [ghost] + [pltpu.roll(t, FIELDS, 0) for t in swap] + [ghost]
        fresh = []
        for j, t in enumerate(tiles):
            beyond = jnp.where(up, turned[j], jnp.where(down, turned[j + 2], turned[j + 1]))
            west = jnp.where(cell == 0, 0.0, pltpu.roll(t, 1, 1))
            east = jnp.where(cell == PC - 1, 0.0, pltpu.roll(t, LANES - 1, 1))
            total = swap[j] + beyond + west + east - 4.0 * t
            fresh.append(t + nu[8 * j:8 * j + 8] * total)
        tiles = fresh
    return jnp.concatenate(tiles, axis=0)


def shards(mesh, fields, new_owner, leaflet, stiffness, coarse, coarse_of_slot, viscosity):
    n_ax, n_az = mesh.shape["axial"], mesh.shape["azim"]
    devices = n_ax * n_az
    patches, _, section = fields.shape
    records, rows, cols = leaflet.shape
    each = max(2, 3 * patches // (2 * devices))
    slots = devices * each
    wide = -(-slots // LANES) * LANES
    height = FIELDS * section // LANES
    part = records // PHASES
    view = fields.reshape(patches, FIELDS, section // LANES, LANES).transpose(0, 2, 1, 3)
    view = view.reshape(patches, height, LANES)
    given = (new_owner.reshape(1, patches), coarse_of_slot, viscosity, view, leaflet, stiffness, coarse)
    out = pl.pallas_call(
        functools.partial(send_kernel, n_ax, n_az, each),
        out_shape=pltpu.VMEM((devices, each, height, LANES), F32),
        in_specs=[pl.BlockSpec(memory_space=pltpu.HBM)] * 7,
        out_specs=pl.BlockSpec(memory_space=pltpu.VMEM),
        scratch_shapes=[
            pltpu.VMEM((1, patches), jnp.int32),
            pltpu.SMEM((slots,), jnp.int32),
            pltpu.SMEM((FIELDS,), F32),
            pltpu.VMEM((patches, height, LANES), F32),
            pltpu.VMEM(leaflet.shape, BF16),
            pltpu.VMEM(stiffness.shape, BF16),
            pltpu.VMEM(coarse.shape, F32),
            pltpu.SemaphoreType.DMA((7,)),
            pltpu.VMEM((2, records, cols), BF16),
            pltpu.VMEM((records, LANES), BF16),
            pltpu.VMEM((2, records, cols), BF16),
            pltpu.VMEM((2, records, LANES), BF16),
            pltpu.VMEM((PHASES, BAND * part, BAND * records), BF16),
            pltpu.VMEM((PHASES, part, LANES), F32),
            pltpu.VMEM((PHASES, rows + 2, part, cols), F32),
            pltpu.VMEM((patches + 1, height, LANES), BF16),
            pltpu.VMEM((devices, each, height, LANES), BF16),
            pltpu.VMEM((devices, each, height, LANES), BF16),
            pltpu.VMEM((coarse.shape[0], 2 * FIELDS, LANES), F32),
            pltpu.VMEM((1, wide), jnp.int32),
            pltpu.SMEM((1, wide), jnp.int32),
            pltpu.SemaphoreType.DMA((4,)),
            pltpu.SemaphoreType.DMA((4,)),
            pltpu.SemaphoreType.DMA((PHASES, devices)),
            pltpu.SemaphoreType.DMA((PHASES, devices)),
            pltpu.SemaphoreType.DMA,
            pltpu.SemaphoreType.REGULAR,
        ],
        compiler_params=pltpu.CompilerParams(
            collective_id=0, has_side_effects=True, vmem_limit_bytes=40 << 20
        ),
        name="regrid",
    )(*[pltpu.with_memory_space_constraint(v, pltpu.HBM) for v in given])
    out = out.reshape(slots, section // LANES, FIELDS, LANES).transpose(0, 2, 1, 3)
    return out.reshape(slots, FIELDS, section)


def solution(mesh):
    placed = (
        P(("axial", "azim"), None, None),
        P(("axial", "azim"), None),
        P(None, "axial", "azim"),
        P(),
        P(("axial", "azim"), None),
        P(("axial", "azim")),
        P(),
    )
    return jax.shard_map(
        functools.partial(shards, mesh),
        mesh=mesh,
        in_specs=placed,
        out_specs=P(("axial", "azim"), None, None),
        check_vma=False,
    )
```

time: 50.3 us -> 48.4 us (0.962); the launches traced: 49.5 us -> 48.3 us
  Pallas kernels: 47.8 us -> 46.6 us
    pallas_call x1, Pallas kernels: 47.8 us -> 46.6 us  [shards(): pl.pallas_call(functools.partial(send_kernel, n_ax, n_az, each), out_shap...]
where the time goes in v1:
time: 48.4 us; the launch traced here: 48.3 us
  Pallas kernels  46.6 us (96%)
  local copies, waits for them, and re-layouts  1.67 us (3%)
    pallas_call x1, Pallas kernels, shards(): pl.pallas_call(functools.partial(send_kernel, n_ax, n_az, each), out_shap...  46.6 us
    unnamed x1, local copies, waits for them, and re-layouts  1.67 us

profile of v1, /device:TPU:11, one launch (start us, length us, event | category | flops | bytes accessed | tf_op | source)
XLA Modules:
  0.0 48.3 jit_solution(13293879307694219351)
XLA Ops:
  0.0 46.6 %regrid.1 = f32[32,6,32,128]{3,2,1,0:T(8,128)S(1)} custom-call(s32[1,128]{1,0:T(1,128)} %bitcast.13, s32[192]{0:T(256)} %slot_hbm.1, f32[4]{0:T(128)} %nu_hbm.1, f32[128,32,128]{2,1,0:T(8,128)} %bitcast.12, bf16[64,32,256]{2,1,0:T(8,128)(2,1)} %leaf_hbm.1, bf16[64,64]{1,0:T(8,128)(2,1)} %stiff_hbm.1, f32[64,256]{1,0:T(8,128)} %coarse_hbm.1), custom_call_target="tpu_custom_call" | custom-call | tf_op jit(solution)/shard_map/regrid/pallas_call | solution.py:394
  46.6 1.7 %copy.11 = f32[192,4,1024]{2,1,0:T(4,128)} copy(f32[192,4,1024]{2,1,0:T(4,128)S(1)} %bitcast.11) | data formatting | bytes 6291456

commit v2 on v1

--- a/solution.py
+++ b/solution.py
@@ -39,9 +39,9 @@
 def send_kernel(
     n_ax, n_az, each, owner_hbm, slot_hbm, nu_hbm, fields_hbm, leaf_hbm, stiff_hbm, coarse_hbm, out_ref,
     owner_ref, slot_ref, nu_ref, fields_ref, leaf_ref, stiff_ref, coarse_ref, load_sem,
-    edge_rows, edge_cols, got_rows, got_cols, law_ref, side_ref, coupled_ref, forced_ref, packed_ref,
+    edge_rows, edge_cols, got_rows, got_cols, lap_ref, law_ref, side_ref, coupled_ref, forced_ref, packed_ref,
     landed_ref, strip_ref, pick_row, pick_ref,
-    halo_send, halo_recv, send_sem, recv_sem, pick_sem, closed_sem,
+    halo_send, halo_recv, send_sem, recv_sem, pick_sem, chain_sem,
 ):
     a = lax.axis_index("axial")
     z = lax.axis_index("azim")
@@ -56,7 +56,7 @@
     wide = 2 * share
 
     pairs_in = (
-        (owner_hbm, owner_ref), (stiff_hbm, stiff_ref), (leaf_hbm, leaf_ref), (fields_hbm, fields_ref),
+        (leaf_hbm, leaf_ref), (owner_hbm, owner_ref), (stiff_hbm, stiff_ref), (fields_hbm, fields_ref),
         (coarse_hbm, coarse_ref), (slot_hbm, slot_ref), (nu_hbm, nu_ref),
     )
     loads = [
@@ -68,9 +68,19 @@
     barrier = pltpu.get_barrier_semaphore()
 
     row_peers = [(a, lax.rem(z + dz, n_az)) for dz in range(1, n_az)]
-    column_peers = [(lax.rem(a + da, n_ax), z) for da in range(1, n_ax)]
-    for other in row_peers + column_peers:
+    for other in row_peers:
         pl.semaphore_signal(barrier, inc=1, device_id=other, device_id_type=MESH)
+
+    above, below = (a + 1, z), (a - 1, z)
+    has_above, has_below = a < n_ax - 1, a > 0
+
+    @pl.when(has_above)
+    def _():
+        pl.semaphore_signal(barrier, inc=1, device_id=above, device_id_type=MESH)
+
+    @pl.when(has_below)
+    def _():
+        pl.semaphore_signal(barrier, inc=1, device_id=below, device_id_type=MESH)
 
     column = iota((records, deep), 1)
     belongs = iota((records, deep), 0) == column // BAND
@@ -81,13 +91,21 @@
     odd_lane = lax.rem(iota((cols, LANES), 1), 2) == 1
     ends = (((source == cols - 1) & ~odd_lane) | ((source == 0) & odd_lane)).astype(BF16)
 
-    loads[0].wait()
+    here_col, there_col = iota((cols, cols), 0), iota((cols, cols), 1)
+    along = (jnp.abs(here_col - there_col) == 1).astype(F32)
+    along = jnp.where(here_col == there_col, -4.0, along).astype(BF16)
+    side = 2 * LANES
+    here_row, there_row = iota((side, side), 0), iota((side, side), 1)
+    upright = (here_row // BAND == there_row // BAND) & (jnp.abs(here_row - there_row) == 1)
+    upright = upright.astype(BF16)
+
+    loads[1].wait()
     pick_slots(each, owner_ref, pick_row)
     picked = pltpu.make_async_copy(pick_row, pick_ref, pick_sem)
     picked.start()
     forced_ref[patches] = jnp.zeros(forced_ref.shape[1:], BF16)
 
-    loads[1].wait()
+    loads[2].wait()
     spread = jnp.dot(stiff_ref[...], gather, preferred_element_type=F32).astype(BF16)
     row_of = lax.rem(iota((wide, deep), 1), BAND)
     small = []
@@ -107,7 +125,7 @@
 
         lax.fori_loop(0, BAND, fill, 0, unroll=2)
 
-    loads[2].wait()
+    loads[0].wait()
     band_lane = iota((BAND, LANES), 1)
     band_row = iota((BAND, LANES), 0)
 
@@ -118,16 +136,40 @@
     for b in range(blocks):
         both = jnp.dot(band(b), ends, preferred_element_type=F32).reshape(records, BAND, LANES)
         twice = 2 * (band_row + b * BAND)
-        kept = (band_lane == twice) | (band_lane == lax.rem(twice + LANES - 1, LANES))
+        kept = (band_lane == twice) | (band_lane == lax.rem(twice + PC - 1, LANES))
         both = jnp.where(kept[None], both, 0.0).astype(BF16).reshape(deep, LANES)
         total = total + jnp.dot(gather, both, preferred_element_type=F32)
     edge_cols[...] = total.astype(BF16)
-    edge_rows[0] = jnp.dot(gather_first, band(0), preferred_element_type=F32).astype(BF16)
-    edge_rows[1] = jnp.dot(gather_last, band(blocks - 1), preferred_element_type=F32).astype(BF16)
-
-    pl.semaphore_wait(barrier, len(row_peers) + len(column_peers))
-    for other in row_peers:
-        pl.semaphore_signal(closed_sem, inc=1, device_id=other, device_id_type=MESH)
+
+    def edge_row(n):
+        chosen = gather_last if n % 2 else gather_first
+        edge_rows[n] = jnp.dot(chosen, band(n // 2), preferred_element_type=F32).astype(BF16)
+
+    edge_row(0)
+    edge_row(2 * blocks - 1)
+
+    pl.semaphore_wait(barrier, len(row_peers) + has_above.astype(jnp.int32) + has_below.astype(jnp.int32))
+
+    def pass_on(k):
+        if k:
+            @pl.when(a >= k)
+            def _():
+                pl.semaphore_wait(chain_sem.at[0, k - 1], 1)
+
+            @pl.when(a < n_ax - k)
+            def _():
+                pl.semaphore_wait(chain_sem.at[1, k - 1], 1)
+
+        if k < n_ax - 1:
+            @pl.when((a >= k) & has_above)
+            def _():
+                pl.semaphore_signal(chain_sem.at[0, k], inc=1, device_id=above, device_id_type=MESH)
+
+            @pl.when((a < n_ax - k) & has_below)
+            def _():
+                pl.semaphore_signal(chain_sem.at[1, k], inc=1, device_id=below, device_id_type=MESH)
+
+    pass_on(0)
 
     def halo(src, dst, i, device):
         return pltpu.make_async_remote_copy(
@@ -135,7 +177,7 @@
             device_id=device, device_id_type=MESH,
         )
 
-    down = halo(edge_rows.at[1], got_rows.at[0], 0, (lax.rem(a + 1, n_ax), z))
+    down = halo(edge_rows.at[2 * blocks - 1], got_rows.at[0], 0, (lax.rem(a + 1, n_ax), z))
     up = halo(edge_rows.at[0], got_rows.at[1], 1, (lax.rem(a + n_ax - 1, n_ax), z))
     right = halo(edge_cols, got_cols.at[0], 2, (a, lax.rem(z + 1, n_az)))
     left = halo(edge_cols, got_cols.at[1], 3, (a, lax.rem(z + n_az - 1, n_az)))
@@ -151,15 +193,43 @@
     right.start()
     left.start()
 
+    for n in range(1, 2 * blocks - 1):
+        edge_row(n)
+    held = side // BAND
+
+    def laplace(b):
+        def one(c, carry):
+            some = pl.ds(pl.multiple_of(c * held, held), held)
+            x = leaf_ref[some, b * BAND:(b + 1) * BAND, :].reshape(side, cols)
+            total = jnp.dot(x, along, preferred_element_type=F32)
+            total = total + jnp.dot(upright, x, preferred_element_type=F32)
+            lap_ref[b, pl.ds(pl.multiple_of(c * side, side), side), :] = total.astype(BF16)
+            return carry
+
+        lax.fori_loop(0, deep // side, one, 0, unroll=2)
+
+    for b in range(blocks):
+        laplace(b)
+
     def couple(h):
         def one(b, carry):
-            found = jnp.dot(law_ref[h], band(b), preferred_element_type=F32)
-            coupled_ref[h, pl.ds(1 + b * BAND, BAND)] = found.reshape(BAND, wide, cols)
+            found = jnp.dot(law_ref[h], lap_ref[b], preferred_element_type=F32)
+            coupled_ref[h, pl.ds(pl.multiple_of(b * BAND, BAND), BAND)] = found.reshape(BAND, wide, cols)
             return carry
 
         lax.fori_loop(0, blocks, one, 0)
-
+        for b in range(1, blocks):
+            add_row(h, b * BAND - 1, edge_rows[2 * b])
+            add_row(h, b * BAND, edge_rows[2 * b - 1])
+
+    def add_row(h, r, record_row):
+        coupled_ref[h, r] += jnp.dot(small[h], record_row, preferred_element_type=F32)
+
+    near = n_ax - 1 if n_ax & (n_ax - 1) else n_ax // 2
+    pass_on(1)
     couple(0)
+    for k in range(2, near + 1):
+        pass_on(k)
 
     @pl.when(a > 0)
     def _():
@@ -176,15 +246,13 @@
 
     def border(h):
         side_ref[h] = jnp.dot(small[h], beside, preferred_element_type=F32)
-        coupled_ref[h, 0] = jnp.dot(small[h], got_rows[0], preferred_element_type=F32)
-        coupled_ref[h, rows + 1] = jnp.dot(small[h], got_rows[1], preferred_element_type=F32)
+        add_row(h, 0, got_rows[0])
+        add_row(h, rows - 1, got_rows[1])
 
     border(0)
 
-    lane = iota((wide, LANES), 1)
-    first_lane = lane == 0
-    last_lane = lane == LANES - 1
-    low = iota((share, LANES), 1) < PC
+    lane = iota((share, LANES), 1)
+    low = lane < PC
     across = cols // PC
     tiles = cols // LANES
 
@@ -194,22 +262,20 @@
         def some(turn, carry):
             stored = []
             for r in [turn * TOGETHER + n for n in range(TOGETHER)]:
-                beyond = pltpu.roll(side_ref[h], lax.rem(2 * LANES - 2 * r, LANES), 1)
-                here = [coupled_ref[h, r + 1, :, t * LANES:(t + 1) * LANES] for t in range(tiles)]
-                west = [pltpu.roll(v, 1, 1) for v in here]
-                east = [pltpu.roll(v, LANES - 1, 1) for v in here]
+                over = pltpu.roll(side_ref[h, :share], lax.rem(2 * LANES - 2 * r, LANES), 1)
+                under = pltpu.roll(side_ref[h, share:], lax.rem(2 * LANES + PC - 2 * r, LANES), 1)
                 for t in range(tiles):
                     cut = slice(t * LANES, (t + 1) * LANES)
-                    before = west[t - 1] if t else beyond
-                    after = east[t + 1] if t < tiles - 1 else beyond
-                    sums = jnp.where(first_lane, before, west[t]) + jnp.where(last_lane, after, east[t])
-                    sums = sums + (coupled_ref[h, r, :, cut] + coupled_ref[h, r + 2, :, cut])
-                    change = SPREAD * sums - (4.0 * SPREAD) * here[t]
-                    top, bottom = change[:share], change[share:]
+                    top, bottom = coupled_ref[h, r, :share, cut], coupled_ref[h, r, share:, cut]
                     turned = pltpu.roll(jnp.where(low, bottom, top), PC, 1)
+                    one, two = jnp.where(low, top, turned), jnp.where(low, turned, bottom)
+                    if t == 0:
+                        one = one + jnp.where(lane == 0, over, jnp.where(lane == PC, under, 0.0))
+                    if t == tiles - 1:
+                        two = two + jnp.where(lane == PC - 1, over, jnp.where(lane == LANES - 1, under, 0.0))
                     p = r * across + 2 * t
-                    stored.append((p, (fields_ref[p, part] + jnp.where(low, top, turned)).astype(BF16)))
-                    stored.append((p + 1, (fields_ref[p + 1, part] + jnp.where(low, turned, bottom)).astype(BF16)))
+                    stored.append((p, (fields_ref[p, part] + SPREAD * one).astype(BF16)))
+                    stored.append((p + 1, (fields_ref[p + 1, part] + SPREAD * two).astype(BF16)))
             for p, value in stored:
                 forced_ref[p, part] = value
             return carry
@@ -256,8 +322,9 @@
     loads[3].wait()
     force(0)
     picked.wait()
-    pl.semaphore_wait(closed_sem, len(row_peers))
     send_all(0, 0)
+    for k in range(near + 1, n_ax):
+        pass_on(k)
     for h in range(1, PHASES):
         couple(h)
         border(h)
@@ -405,13 +472,14 @@
             pltpu.VMEM(stiffness.shape, BF16),
             pltpu.VMEM(coarse.shape, F32),
             pltpu.SemaphoreType.DMA((7,)),
-            pltpu.VMEM((2, records, cols), BF16),
+            pltpu.VMEM((2 * rows // BAND, records, cols), BF16),
             pltpu.VMEM((records, LANES), BF16),
             pltpu.VMEM((2, records, cols), BF16),
             pltpu.VMEM((2, records, LANES), BF16),
+            pltpu.VMEM((rows // BAND, BAND * records, cols), BF16),
             pltpu.VMEM((PHASES, BAND * part, BAND * records), BF16),
             pltpu.VMEM((PHASES, part, LANES), F32),
-            pltpu.VMEM((PHASES, rows + 2, part, cols), F32),
+            pltpu.VMEM((PHASES, rows, part, cols), F32),
             pltpu.VMEM((patches + 1, height, LANES), BF16),
             pltpu.VMEM((devices, each, height, LANES), BF16),
             pltpu.VMEM((devices, each, height, LANES), BF16),
@@ -423,7 +491,7 @@
             pltpu.SemaphoreType.DMA((PHASES, devices)),
             pltpu.SemaphoreType.DMA((PHASES, devices)),
             pltpu.SemaphoreType.DMA,
-            pltpu.SemaphoreType.REGULAR,
+            pltpu.SemaphoreType.REGULAR((2, n_ax - 1)),
         ],
         compiler_params=pltpu.CompilerParams(
             collective_id=0, has_side_effects=True, vmem_limit_bytes=40 << 20

time: 48.4 us -> 47.6 us (0.983)
  Pallas kernels: 46.6 us -> 45.8 us
    pallas_call x1, Pallas kernels: 46.6 us -> 45.8 us  [shards(): pl.pallas_call(functools.partial(send_kernel, n_ax, n_az, each), out_shap...]
where the time goes in v2:
time: 47.6 us; the launch traced here: 47.4 us
  Pallas kernels  45.8 us (96%)
  local copies, waits for them, and re-layouts  1.67 us (4%)
    pallas_call x1, Pallas kernels, shards(): pl.pallas_call(functools.partial(send_kernel, n_ax, n_az, each), out_shap...  45.8 us
    unnamed x1, local copies, waits for them, and re-layouts  1.67 us

profile of v2, /device:TPU:11, one launch (start us, length us, event | category | flops | bytes accessed | tf_op | source)
XLA Modules:
  0.0 47.4 jit_solution(15927825729061134697)
XLA Ops:
  0.0 45.8 %regrid.1 = f32[32,6,32,128]{3,2,1,0:T(8,128)S(1)} custom-call(s32[1,128]{1,0:T(1,128)} %bitcast.13, s32[192]{0:T(256)} %slot_hbm.1, f32[4]{0:T(128)} %nu_hbm.1, f32[128,32,128]{2,1,0:T(8,128)} %bitcast.12, bf16[64,32,256]{2,1,0:T(8,128)(2,1)} %leaf_hbm.1, bf16[64,64]{1,0:T(8,128)(2,1)} %stiff_hbm.1, f32[64,256]{1,0:T(8,128)} %coarse_hbm.1), custom_call_target="tpu_custom_call" | custom-call | tf_op jit(solution)/shard_map/regrid/pallas_call | solution.py:461
  45.8 1.7 %copy.11 = f32[192,4,1024]{2,1,0:T(4,128)} copy(f32[192,4,1024]{2,1,0:T(4,128)S(1)} %bitcast.11) | data formatting | bytes 6291456

commit v3 on v2

--- a/solution.py
+++ b/solution.py
@@ -10,9 +10,9 @@
 FIELDS = 4
 STEPS = 2
 SPREAD = 0.25
-PHASES = 2
+FIRST = 8
 BAND = 16
-TOGETHER = 4
+TOGETHER = (8, 4)
 LANES = 128
 MESH = pl.DeviceIdType.MESH
 F32 = jnp.float32
@@ -52,8 +52,7 @@
     blocks = rows // BAND
     deep = records * BAND
     pairs = records // FIELDS // 2
-    share = pairs // PHASES * FIELDS
-    wide = 2 * share
+    cuts = ((0, FIRST), (FIRST, height - FIRST))
 
     pairs_in = (
         (leaf_hbm, leaf_ref), (owner_hbm, owner_ref), (stiff_hbm, stiff_ref), (fields_hbm, fields_ref),
@@ -91,40 +90,6 @@
     odd_lane = lax.rem(iota((cols, LANES), 1), 2) == 1
     ends = (((source == cols - 1) & ~odd_lane) | ((source == 0) & odd_lane)).astype(BF16)
 
-    here_col, there_col = iota((cols, cols), 0), iota((cols, cols), 1)
-    along = (jnp.abs(here_col - there_col) == 1).astype(F32)
-    along = jnp.where(here_col == there_col, -4.0, along).astype(BF16)
-    side = 2 * LANES
-    here_row, there_row = iota((side, side), 0), iota((side, side), 1)
-    upright = (here_row // BAND == there_row // BAND) & (jnp.abs(here_row - there_row) == 1)
-    upright = upright.astype(BF16)
-
-    loads[1].wait()
-    pick_slots(each, owner_ref, pick_row)
-    picked = pltpu.make_async_copy(pick_row, pick_ref, pick_sem)
-    picked.start()
-    forced_ref[patches] = jnp.zeros(forced_ref.shape[1:], BF16)
-
-    loads[2].wait()
-    spread = jnp.dot(stiff_ref[...], gather, preferred_element_type=F32).astype(BF16)
-    row_of = lax.rem(iota((wide, deep), 1), BAND)
-    small = []
-    for h in range(PHASES):
-        order = iota((wide, records), 0)
-        within = lax.rem(order, share)
-        wanted = lax.rem(within, FIELDS) * (2 * pairs) + order // share
-        wanted = wanted + 2 * (h * (pairs // PHASES) + within // FIELDS)
-        chosen = (iota((wide, records), 1) == wanted).astype(BF16)
-        small.append(jnp.dot(chosen, stiff_ref[...], preferred_element_type=F32).astype(BF16))
-        base = jnp.dot(chosen, spread, preferred_element_type=F32)
-
-        def fill(r, carry, h=h, base=base):
-            here = pl.ds(pl.multiple_of(r * wide, wide), wide)
-            law_ref[h, here, :] = jnp.where(row_of == r, base, 0.0).astype(BF16)
-            return carry
-
-        lax.fori_loop(0, BAND, fill, 0, unroll=2)
-
     loads[0].wait()
     band_lane = iota((BAND, LANES), 1)
     band_row = iota((BAND, LANES), 0)
@@ -141,13 +106,6 @@
         total = total + jnp.dot(gather, both, preferred_element_type=F32)
     edge_cols[...] = total.astype(BF16)
 
-    def edge_row(n):
-        chosen = gather_last if n % 2 else gather_first
-        edge_rows[n] = jnp.dot(chosen, band(n // 2), preferred_element_type=F32).astype(BF16)
-
-    edge_row(0)
-    edge_row(2 * blocks - 1)
-
     pl.semaphore_wait(barrier, len(row_peers) + has_above.astype(jnp.int32) + has_below.astype(jnp.int32))
 
     def pass_on(k):
@@ -182,17 +140,62 @@
     right = halo(edge_cols, got_cols.at[0], 2, (a, lax.rem(z + 1, n_az)))
     left = halo(edge_cols, got_cols.at[1], 3, (a, lax.rem(z + n_az - 1, n_az)))
 
-    @pl.when(a < n_ax - 1)
-    def _():
-        down.start()
-
-    @pl.when(a > 0)
-    def _():
-        up.start()
-
     right.start()
     left.start()
 
+    def edge_row(n):
+        chosen = gather_last if n % 2 else gather_first
+        edge_rows[n] = jnp.dot(chosen, band(n // 2), preferred_element_type=F32).astype(BF16)
+
+    edge_row(0)
+    edge_row(2 * blocks - 1)
+
+    @pl.when(a < n_ax - 1)
+    def _():
+        down.start()
+
+    @pl.when(a > 0)
+    def _():
+        up.start()
+
+    here_col, there_col = iota((cols, cols), 0), iota((cols, cols), 1)
+    along = (jnp.abs(here_col - there_col) == 1).astype(F32)
+    along = jnp.where(here_col == there_col, -4.0, along).astype(BF16)
+    side = 2 * LANES
+    here_row, there_row = iota((side, side), 0), iota((side, side), 1)
+    upright = (here_row // BAND == there_row // BAND) & (jnp.abs(here_row - there_row) == 1)
+    upright = upright.astype(BF16)
+
+    loads[1].wait()
+    pick_slots(each, owner_ref, pick_row)
+    picked = pltpu.make_async_copy(pick_row, pick_ref, pick_sem)
+    picked.start()
+    forced_ref[patches] = jnp.zeros(forced_ref.shape[1:], BF16)
+
+    loads[2].wait()
+    spread = jnp.dot(stiff_ref[...], gather, preferred_element_type=F32).astype(BF16)
+    small = []
+
+    def build(h):
+        start, share = cuts[h]
+        wide = 2 * share
+        row_of = lax.rem(iota((wide, deep), 1), BAND)
+        order = iota((wide, records), 0)
+        within = lax.rem(order, share)
+        wanted = lax.rem(within, FIELDS) * (2 * pairs) + order // share
+        wanted = wanted + 2 * (start // FIELDS + within // FIELDS)
+        chosen = (iota((wide, records), 1) == wanted).astype(BF16)
+        small.append(jnp.dot(chosen, stiff_ref[...], preferred_element_type=F32).astype(BF16))
+        base = jnp.dot(chosen, spread, preferred_element_type=F32)
+
+        def fill(r, carry):
+            here = pl.ds(pl.multiple_of(2 * BAND * start + r * wide, 16), wide)
+            law_ref[here, :] = jnp.where(row_of == r, base, 0.0).astype(BF16)
+            return carry
+
+        lax.fori_loop(0, BAND, fill, 0, unroll=2)
+
+    build(0)
     for n in range(1, 2 * blocks - 1):
         edge_row(n)
     held = side // BAND
@@ -211,10 +214,17 @@
     for b in range(blocks):
         laplace(b)
 
+    def rows_of(h):
+        start, share = cuts[h]
+        return slice(2 * start, 2 * (start + share))
+
     def couple(h):
+        start, share = cuts[h]
+
         def one(b, carry):
-            found = jnp.dot(law_ref[h], lap_ref[b], preferred_element_type=F32)
-            coupled_ref[h, pl.ds(pl.multiple_of(b * BAND, BAND), BAND)] = found.reshape(BAND, wide, cols)
+            law = law_ref[2 * BAND * start:2 * BAND * (start + share), :]
+            found = jnp.dot(law, lap_ref[b], preferred_element_type=F32).reshape(BAND, 2 * share, cols)
+            coupled_ref[pl.ds(pl.multiple_of(b * BAND, BAND), BAND), rows_of(h), :] = found
             return carry
 
         lax.fori_loop(0, blocks, one, 0)
@@ -223,7 +233,7 @@
             add_row(h, b * BAND, edge_rows[2 * b - 1])
 
     def add_row(h, r, record_row):
-        coupled_ref[h, r] += jnp.dot(small[h], record_row, preferred_element_type=F32)
+        coupled_ref[r, rows_of(h), :] += jnp.dot(small[h], record_row, preferred_element_type=F32)
 
     near = n_ax - 1 if n_ax & (n_ax - 1) else n_ax // 2
     pass_on(1)
@@ -245,28 +255,31 @@
     beside = jnp.where(even, got_cols[0].astype(F32), got_cols[1].astype(F32)).astype(BF16)
 
     def border(h):
-        side_ref[h] = jnp.dot(small[h], beside, preferred_element_type=F32)
+        side_ref[rows_of(h), :] = jnp.dot(small[h], beside, preferred_element_type=F32)
         add_row(h, 0, got_rows[0])
         add_row(h, rows - 1, got_rows[1])
 
     border(0)
 
-    lane = iota((share, LANES), 1)
-    low = lane < PC
     across = cols // PC
     tiles = cols // LANES
 
     def force(h):
-        part = slice(h * share, (h + 1) * share)
+        start, share = cuts[h]
+        part = slice(start, start + share)
+        upper, lower = slice(2 * start, 2 * start + share), slice(2 * start + share, 2 * (start + share))
+        lane = iota((share, LANES), 1)
+        low = lane < PC
+        together = TOGETHER[h]
 
         def some(turn, carry):
             stored = []
-            for r in [turn * TOGETHER + n for n in range(TOGETHER)]:
-                over = pltpu.roll(side_ref[h, :share], lax.rem(2 * LANES - 2 * r, LANES), 1)
-                under = pltpu.roll(side_ref[h, share:], lax.rem(2 * LANES + PC - 2 * r, LANES), 1)
+            for r in [turn * together + n for n in range(together)]:
+                over = pltpu.roll(side_ref[upper, :], lax.rem(2 * LANES - 2 * r, LANES), 1)
+                under = pltpu.roll(side_ref[lower, :], lax.rem(2 * LANES + PC - 2 * r, LANES), 1)
                 for t in range(tiles):
                     cut = slice(t * LANES, (t + 1) * LANES)
-                    top, bottom = coupled_ref[h, r, :share, cut], coupled_ref[h, r, share:, cut]
+                    top, bottom = coupled_ref[r, upper, cut], coupled_ref[r, lower, cut]
                     turned = pltpu.roll(jnp.where(low, bottom, top), PC, 1)
                     one, two = jnp.where(low, top, turned), jnp.where(low, turned, bottom)
                     if t == 0:
@@ -280,13 +293,13 @@
                 forced_ref[p, part] = value
             return carry
 
-        lax.fori_loop(0, rows // TOGETHER, some, 0)
+        lax.fori_loop(0, rows // together, some, 0)
 
     order = shifts(n_ax)
     turns = [n_az - (shift == 0) for shift in order]
 
     def piece(ref, at, h):
-        return ref.at[at] if h is None else ref.at[at, :, h * share:(h + 1) * share]
+        return ref.at[at] if h is None else ref.at[at, :, cuts[h][0]:sum(cuts[h])]
 
     def outgoing(j, d, h=None):
         ta, tz = partner(a, order[j], n_ax), lax.rem(z + d + 1, n_az)
@@ -306,7 +319,7 @@
         )
 
     def send_all(j, h=None):
-        part = slice(None) if h is None else slice(h * share, (h + 1) * share)
+        part = slice(None) if h is None else slice(cuts[h][0], sum(cuts[h]))
 
         def send(d, carry):
             other, copy = outgoing(j, d, h)
@@ -317,19 +330,20 @@
 
         lax.fori_loop(0, turns[j], send, 0)
 
-    halves = [range(PHASES) if j == 0 else (None,) for j in range(n_ax)]
+    halves = [range(len(cuts)) if j == 0 else (None,) for j in range(n_ax)]
 
     loads[3].wait()
     force(0)
     picked.wait()
     send_all(0, 0)
-    for k in range(near + 1, n_ax):
-        pass_on(k)
-    for h in range(1, PHASES):
+    for h in range(1, len(cuts)):
+        build(h)
         couple(h)
         border(h)
         force(h)
         send_all(0, h)
+    for k in range(near + 1, n_ax):
+        pass_on(k)
     for j in range(1, n_ax):
         send_all(j)
 
@@ -454,7 +468,6 @@
     slots = devices * each
     wide = -(-slots // LANES) * LANES
     height = FIELDS * section // LANES
-    part = records // PHASES
     view = fields.reshape(patches, FIELDS, section // LANES, LANES).transpose(0, 2, 1, 3)
     view = view.reshape(patches, height, LANES)
     given = (new_owner.reshape(1, patches), coarse_of_slot, viscosity, view, leaflet, stiffness, coarse)
@@ -477,9 +490,9 @@
             pltpu.VMEM((2, records, cols), BF16),
             pltpu.VMEM((2, records, LANES), BF16),
             pltpu.VMEM((rows // BAND, BAND * records, cols), BF16),
-            pltpu.VMEM((PHASES, BAND * part, BAND * records), BF16),
-            pltpu.VMEM((PHASES, part, LANES), F32),
-            pltpu.VMEM((PHASES, rows, part, cols), F32),
+            pltpu.VMEM((BAND * records, BAND * records), BF16),
+            pltpu.VMEM((records, LANES), F32),
+            pltpu.VMEM((rows, records, cols), F32),
             pltpu.VMEM((patches + 1, height, LANES), BF16),
             pltpu.VMEM((devices, each, height, LANES), BF16),
             pltpu.VMEM((devices, each, height, LANES), BF16),
@@ -488,8 +501,8 @@
             pltpu.SMEM((1, wide), jnp.int32),
             pltpu.SemaphoreType.DMA((4,)),
             pltpu.SemaphoreType.DMA((4,)),
-            pltpu.SemaphoreType.DMA((PHASES, devices)),
-            pltpu.SemaphoreType.DMA((PHASES, devices)),
+            pltpu.SemaphoreType.DMA((2, devices)),
+            pltpu.SemaphoreType.DMA((2, devices)),
             pltpu.SemaphoreType.DMA,
             pltpu.SemaphoreType.REGULAR((2, n_ax - 1)),
         ],

time: 47.6 us -> 46.2 us (0.971)
  Pallas kernels: 45.8 us -> 44.1 us
    pallas_call x1, Pallas kernels: 45.8 us -> 44.1 us  [shards(): pl.pallas_call(functools.partial(send_kernel, n_ax, n_az, each), out_shap...]
where the time goes in v3:
time: 46.2 us; the launch traced here: 45.8 us
  Pallas kernels  44.1 us (95%)
  local copies, waits for them, and re-layouts  1.67 us (4%)
    pallas_call x1, Pallas kernels, shards(): pl.pallas_call(functools.partial(send_kernel, n_ax, n_az, each), out_shap...  44.1 us
    unnamed x1, local copies, waits for them, and re-layouts  1.67 us

profile of v3, /device:TPU:11, one launch (start us, length us, event | category | flops | bytes accessed | tf_op | source)
XLA Modules:
  0.0 45.8 jit_solution(18287400722300812709)
XLA Ops:
  0.0 44.1 %regrid.1 = f32[32,6,32,128]{3,2,1,0:T(8,128)S(1)} custom-call(s32[1,128]{1,0:T(1,128)} %bitcast.13, s32[192]{0:T(256)} %slot_hbm.1, f32[4]{0:T(128)} %nu_hbm.1, f32[128,32,128]{2,1,0:T(8,128)} %bitcast.12, bf16[64,32,256]{2,1,0:T(8,128)(2,1)} %leaf_hbm.1, bf16[64,64]{1,0:T(8,128)(2,1)} %stiff_hbm.1, f32[64,256]{1,0:T(8,128)} %coarse_hbm.1), custom_call_target="tpu_custom_call" | custom-call | tf_op jit(solution)/shard_map/regrid/pallas_call | solution.py:474
  44.1 1.7 %copy.11 = f32[192,4,1024]{2,1,0:T(4,128)} copy(f32[192,4,1024]{2,1,0:T(4,128)S(1)} %bitcast.11) | data formatting | bytes 6291456

commit v4 on v3

--- a/solution.py
+++ b/solution.py
@@ -347,6 +347,17 @@
     for j in range(1, n_ax):
         send_all(j)
 
+    @pl.when(a < n_ax - 1)
+    def _():
+        down.wait_send()
+
+    @pl.when(a > 0)
+    def _():
+        up.wait_send()
+
+    right.wait_send()
+    left.wait_send()
+
     for load in loads[4:]:
         load.wait()
     interpolate(coarse_ref, strip_ref)
@@ -368,32 +379,28 @@
             ghost = strip_ref[slot_ref[source * each + k]]
             out_ref[source, k] = relax(landed_ref[source, k].astype(F32), ghost, nu)
 
+    def finish(j):
+        def one(d, carry):
+            for h in halves[j]:
+                outgoing(j, d, h)[1].wait_send()
+            return carry
+
+        lax.fori_loop(0, turns[j], one, 0)
+
     far = n_ax // 2
-    for j in sorted(range(n_ax), key=lambda j: (order[j] > 0, order[j] != far, order[j] > far, -order[j])):
+    visits = sorted(range(n_ax), key=lambda j: (order[j] > 0, order[j] != far, order[j] > far, -order[j]))
+    for j in visits:
+        if j == visits[-1]:
+            for other in visits[:-1]:
+                finish(other)
+
         def one(d, carry, j=j):
             arrive(j, d)
             return carry
 
         lax.fori_loop(0, turns[j], one, 0)
 
-    for j in range(n_ax):
-        def finish(d, carry, j=j):
-            for h in halves[j]:
-                outgoing(j, d, h)[1].wait_send()
-            return carry
-
-        lax.fori_loop(0, turns[j], finish, 0)
-
-    @pl.when(a < n_ax - 1)
-    def _():
-        down.wait_send()
-
-    @pl.when(a > 0)
-    def _():
-        up.wait_send()
-
-    right.wait_send()
-    left.wait_send()
+    finish(visits[-1])
 
 
 def pick_slots(each, owner_ref, pick_row):

time: 46.2 us -> 46.1 us (level)
  no operation moved by 1% of the time
where the time goes in v4:
time: 46.1 us; the launch traced here: 45.6 us
  Pallas kernels  43.9 us (95%)
  local copies, waits for them, and re-layouts  1.67 us (4%)
    pallas_call x1, Pallas kernels, shards(): pl.pallas_call(functools.partial(send_kernel, n_ax, n_az, each), out_shap...  43.9 us
    unnamed x1, local copies, waits for them, and re-layouts  1.67 us

profile of v4, /device:TPU:11, one launch (start us, length us, event | category | flops | bytes accessed | tf_op | source)
XLA Modules:
  0.0 45.6 jit_solution(11429934286420901949)
XLA Ops:
  0.0 43.9 %regrid.1 = f32[32,6,32,128]{3,2,1,0:T(8,128)S(1)} custom-call(s32[1,128]{1,0:T(1,128)} %bitcast.13, s32[192]{0:T(256)} %slot_hbm.1, f32[4]{0:T(128)} %nu_hbm.1, f32[128,32,128]{2,1,0:T(8,128)} %bitcast.12, bf16[64,32,256]{2,1,0:T(8,128)(2,1)} %leaf_hbm.1, bf16[64,64]{1,0:T(8,128)(2,1)} %stiff_hbm.1, f32[64,256]{1,0:T(8,128)} %coarse_hbm.1), custom_call_target="tpu_custom_call" | custom-call | tf_op jit(solution)/shard_map/regrid/pallas_call | solution.py:481
  43.9 1.7 %copy.11 = f32[192,4,1024]{2,1,0:T(4,128)} copy(f32[192,4,1024]{2,1,0:T(4,128)S(1)} %bitcast.11) | data formatting | bytes 6291456

commit v5 on v4

--- a/solution.py
+++ b/solution.py
@@ -90,74 +90,6 @@
     odd_lane = lax.rem(iota((cols, LANES), 1), 2) == 1
     ends = (((source == cols - 1) & ~odd_lane) | ((source == 0) & odd_lane)).astype(BF16)
 
-    loads[0].wait()
-    band_lane = iota((BAND, LANES), 1)
-    band_row = iota((BAND, LANES), 0)
-
-    def band(b):
-        return leaf_ref[:, pl.ds(pl.multiple_of(b * BAND, BAND), BAND), :].reshape(deep, cols)
-
-    total = jnp.zeros((records, LANES), F32)
-    for b in range(blocks):
-        both = jnp.dot(band(b), ends, preferred_element_type=F32).reshape(records, BAND, LANES)
-        twice = 2 * (band_row + b * BAND)
-        kept = (band_lane == twice) | (band_lane == lax.rem(twice + PC - 1, LANES))
-        both = jnp.where(kept[None], both, 0.0).astype(BF16).reshape(deep, LANES)
-        total = total + jnp.dot(gather, both, preferred_element_type=F32)
-    edge_cols[...] = total.astype(BF16)
-
-    pl.semaphore_wait(barrier, len(row_peers) + has_above.astype(jnp.int32) + has_below.astype(jnp.int32))
-
-    def pass_on(k):
-        if k:
-            @pl.when(a >= k)
-            def _():
-                pl.semaphore_wait(chain_sem.at[0, k - 1], 1)
-
-            @pl.when(a < n_ax - k)
-            def _():
-                pl.semaphore_wait(chain_sem.at[1, k - 1], 1)
-
-        if k < n_ax - 1:
-            @pl.when((a >= k) & has_above)
-            def _():
-                pl.semaphore_signal(chain_sem.at[0, k], inc=1, device_id=above, device_id_type=MESH)
-
-            @pl.when((a < n_ax - k) & has_below)
-            def _():
-                pl.semaphore_signal(chain_sem.at[1, k], inc=1, device_id=below, device_id_type=MESH)
-
-    pass_on(0)
-
-    def halo(src, dst, i, device):
-        return pltpu.make_async_remote_copy(
-            src_ref=src, dst_ref=dst, send_sem=halo_send.at[i], recv_sem=halo_recv.at[i],
-            device_id=device, device_id_type=MESH,
-        )
-
-    down = halo(edge_rows.at[2 * blocks - 1], got_rows.at[0], 0, (lax.rem(a + 1, n_ax), z))
-    up = halo(edge_rows.at[0], got_rows.at[1], 1, (lax.rem(a + n_ax - 1, n_ax), z))
-    right = halo(edge_cols, got_cols.at[0], 2, (a, lax.rem(z + 1, n_az)))
-    left = halo(edge_cols, got_cols.at[1], 3, (a, lax.rem(z + n_az - 1, n_az)))
-
-    right.start()
-    left.start()
-
-    def edge_row(n):
-        chosen = gather_last if n % 2 else gather_first
-        edge_rows[n] = jnp.dot(chosen, band(n // 2), preferred_element_type=F32).astype(BF16)
-
-    edge_row(0)
-    edge_row(2 * blocks - 1)
-
-    @pl.when(a < n_ax - 1)
-    def _():
-        down.start()
-
-    @pl.when(a > 0)
-    def _():
-        up.start()
-
     here_col, there_col = iota((cols, cols), 0), iota((cols, cols), 1)
     along = (jnp.abs(here_col - there_col) == 1).astype(F32)
     along = jnp.where(here_col == there_col, -4.0, along).astype(BF16)
@@ -165,12 +97,6 @@
     here_row, there_row = iota((side, side), 0), iota((side, side), 1)
     upright = (here_row // BAND == there_row // BAND) & (jnp.abs(here_row - there_row) == 1)
     upright = upright.astype(BF16)
-
-    loads[1].wait()
-    pick_slots(each, owner_ref, pick_row)
-    picked = pltpu.make_async_copy(pick_row, pick_ref, pick_sem)
-    picked.start()
-    forced_ref[patches] = jnp.zeros(forced_ref.shape[1:], BF16)
 
     loads[2].wait()
     spread = jnp.dot(stiff_ref[...], gather, preferred_element_type=F32).astype(BF16)
@@ -196,6 +122,80 @@
         lax.fori_loop(0, BAND, fill, 0, unroll=2)
 
     build(0)
+    loads[0].wait()
+    band_lane = iota((BAND, LANES), 1)
+    band_row = iota((BAND, LANES), 0)
+
+    def band(b):
+        return leaf_ref[:, pl.ds(pl.multiple_of(b * BAND, BAND), BAND), :].reshape(deep, cols)
+
+    total = jnp.zeros((records, LANES), F32)
+    for b in range(blocks):
+        both = jnp.dot(band(b), ends, preferred_element_type=F32).reshape(records, BAND, LANES)
+        twice = 2 * (band_row + b * BAND)
+        kept = (band_lane == twice) | (band_lane == lax.rem(twice + PC - 1, LANES))
+        both = jnp.where(kept[None], both, 0.0).astype(BF16).reshape(deep, LANES)
+        total = total + jnp.dot(gather, both, preferred_element_type=F32)
+    edge_cols[...] = total.astype(BF16)
+
+    pl.semaphore_wait(barrier, len(row_peers) + has_above.astype(jnp.int32) + has_below.astype(jnp.int32))
+
+    def pass_on(k):
+        if k:
+            @pl.when(a >= k)
+            def _():
+                pl.semaphore_wait(chain_sem.at[0, k - 1], 1)
+
+            @pl.when(a < n_ax - k)
+            def _():
+                pl.semaphore_wait(chain_sem.at[1, k - 1], 1)
+
+        if k < n_ax - 1:
+            @pl.when((a >= k) & has_above)
+            def _():
+                pl.semaphore_signal(chain_sem.at[0, k], inc=1, device_id=above, device_id_type=MESH)
+
+            @pl.when((a < n_ax - k) & has_below)
+            def _():
+                pl.semaphore_signal(chain_sem.at[1, k], inc=1, device_id=below, device_id_type=MESH)
+
+    pass_on(0)
+
+    def halo(src, dst, i, device):
+        return pltpu.make_async_remote_copy(
+            src_ref=src, dst_ref=dst, send_sem=halo_send.at[i], recv_sem=halo_recv.at[i],
+            device_id=device, device_id_type=MESH,
+        )
+
+    down = halo(edge_rows.at[2 * blocks - 1], got_rows.at[0], 0, (lax.rem(a + 1, n_ax), z))
+    up = halo(edge_rows.at[0], got_rows.at[1], 1, (lax.rem(a + n_ax - 1, n_ax), z))
+    right = halo(edge_cols, got_cols.at[0], 2, (a, lax.rem(z + 1, n_az)))
+    left = halo(edge_cols, got_cols.at[1], 3, (a, lax.rem(z + n_az - 1, n_az)))
+
+    right.start()
+    left.start()
+
+    def edge_row(n):
+        chosen = gather_last if n % 2 else gather_first
+        edge_rows[n] = jnp.dot(chosen, band(n // 2), preferred_element_type=F32).astype(BF16)
+
+    edge_row(0)
+    edge_row(2 * blocks - 1)
+
+    @pl.when(a < n_ax - 1)
+    def _():
+        down.start()
+
+    @pl.when(a > 0)
+    def _():
+        up.start()
+
+    loads[1].wait()
+    pick_slots(each, owner_ref, pick_row)
+    picked = pltpu.make_async_copy(pick_row, pick_ref, pick_sem)
+    picked.start()
+    forced_ref[patches] = jnp.zeros(forced_ref.shape[1:], BF16)
+
     for n in range(1, 2 * blocks - 1):
         edge_row(n)
     held = side // BAND

time: 46.1 us -> 45.9 us (level)
  no operation moved by 1% of the time
where the time goes in v5:
time: 45.9 us; the launch traced here: 45.8 us
  Pallas kernels  44.1 us (96%)
  local copies, waits for them, and re-layouts  1.67 us (4%)
    pallas_call x1, Pallas kernels, shards(): pl.pallas_call(functools.partial(send_kernel, n_ax, n_az, each), out_shap...  44.1 us
    unnamed x1, local copies, waits for them, and re-layouts  1.67 us

profile of v5, /device:TPU:11, one launch (start us, length us, event | category | flops | bytes accessed | tf_op | source)
XLA Modules:
  0.0 45.8 jit_solution(4456039310484082060)
XLA Ops:
  0.0 44.1 %regrid.1 = f32[32,6,32,128]{3,2,1,0:T(8,128)S(1)} custom-call(s32[1,128]{1,0:T(1,128)} %bitcast.13, s32[192]{0:T(256)} %slot_hbm.1, f32[4]{0:T(128)} %nu_hbm.1, f32[128,32,128]{2,1,0:T(8,128)} %bitcast.12, bf16[64,32,256]{2,1,0:T(8,128)(2,1)} %leaf_hbm.1, bf16[64,64]{1,0:T(8,128)(2,1)} %stiff_hbm.1, f32[64,256]{1,0:T(8,128)} %coarse_hbm.1), custom_call_target="tpu_custom_call" | custom-call | tf_op jit(solution)/shard_map/regrid/pallas_call | solution.py:481
  44.1 1.7 %copy.11 = f32[192,4,1024]{2,1,0:T(4,128)} copy(f32[192,4,1024]{2,1,0:T(4,128)S(1)} %bitcast.11) | data formatting | bytes 6291456
